TPU v7x, 32 devices: a whole 2x2x4 slice. The times are simulated.
32 devices in a mesh: pop: 2 (over y), ctx: 4 (over z), exp: 2 (over x), tp: 2 (over core).
Axes of the slice: x: 2, y: 2, z: 4, core: 2. Of those that a mesh axis runs over, the one named last changes fastest.
Arguments:
- tokens: bfloat16 [2048, 2688], P(('pop', 'ctx', 'tp')), parts along dimension 0, may hold values from -6 to 6
- routes: int32 [2048, 6], P(('pop', 'ctx', 'tp')), parts along dimension 0, may hold values from 0 to 15, all different within a row; in each aligned block of 128 rows (0 to 127, 128 to 255, ...) at most 64 rows name the same one
- route_gates: float32 [2048, 6], P(('pop', 'ctx', 'tp')), parts along dimension 0, may hold values from 0.05 to 1
- up_weight: bfloat16 [16, 2688, 1536], P(('ctx', 'tp'), None, 'exp'), may hold values from -0.125 to 0.125
- down_weight: bfloat16 [16, 1536, 2688], P(('ctx', 'tp'), None, 'exp'), may hold values from -0.15625 to 0.15625
- factor_seeds: int32 [32, 4], P(('pop', 'ctx', 'tp')), parts along dimension 0, may hold values from 0 to 15
- up_left: bfloat16 [16, 2688], replicated, may hold values from -0.125 to 0.125
- up_right: bfloat16 [16, 1536], P(None, 'exp'), may hold values from -3 to 3
- down_left: bfloat16 [16, 1536], replicated, may hold values from -0.15625 to 0.15625
- down_right: bfloat16 [16, 2688], P(None, 'exp'), may hold values from -3 to 3
Outputs:
- moe_output: bfloat16 [2048, 2688], P(('pop', 'ctx', 'tp'), 'exp'), parts along dimension 0
There are 2 independent parts, one for each index of `pop`. A program takes and returns all parts, laid end to end along the dimension named above; an argument that names none is the same for every part. Nothing has to cross between parts.
Inputs may be any that keep to these rules, and one draw needn't show every extreme that they name: `routes`: each row names 6 different experts. Among the 128 rows of one device (aligned blocks of 128 rows) no expert is named more than 64 times, and in every draw some expert is named exactly 64 times in some block.
All inputs are finite; a program needn't handle non-finite values.
Results may differ from a plain program's by a relative error of at most 0.0057.
Values may be sent and summed in bfloat16 or wider, within the bound.
A program may use at most 64 MiB of HBM per device.

v0:
```python
import jax
import jax.numpy as jnp
from jax import lax
from jax.sharding import PartitionSpec as P


def pick_rows(factor_table, indices):
    chooser = (
        indices[:, None] == jnp.arange(factor_table.shape[0], dtype=jnp.int32)[None, :]
    ).astype(factor_table.dtype)
    return jnp.dot(chooser, factor_table, preferred_element_type=jnp.float32).astype(
        factor_table.dtype
    )


def on_device(
    tokens,
    routes,
    route_gates,
    up_weight,
    down_weight,
    factor_seeds,
    up_left,
    up_right,
    down_left,
    down_right,
):
    dest_count = lax.axis_size("ctx") * lax.axis_size("tp")
    local_experts = up_weight.shape[0]
    experts_all = dest_count * local_experts
    tok_count, top_count = routes.shape
    capacity = 4 * tok_count * top_count // (3 * experts_all)
    model_width = tokens.shape[1]
    flat_routes = routes.reshape(-1)
    chooser = (flat_routes[:, None] == jnp.arange(experts_all, dtype=jnp.int32)[None, :]).astype(
        jnp.int32
    )
    earlier = jnp.cumsum(chooser, axis=0) - chooser
    slot_index = jnp.sum(earlier * chooser, axis=1)
    target = flat_routes * capacity + slot_index
    pair_token = jnp.arange(tok_count * top_count, dtype=jnp.int32) // top_count + 1
    owner_token = jnp.zeros((experts_all * capacity,), jnp.int32).at[target].set(pair_token)
    source_row = jnp.where(owner_token > 0, owner_token - 1, tok_count)
    padded_tokens = jnp.concatenate([tokens, jnp.zeros((1, model_width), tokens.dtype)], axis=0)
    token_rows = padded_tokens[source_row]
    outgoing = token_rows.reshape(dest_count, local_experts, capacity, model_width)
    left_up = pick_rows(up_left, factor_seeds[:, 0])
    right_up = pick_rows(up_right, factor_seeds[:, 1])
    left_down = pick_rows(down_left, factor_seeds[:, 2])
    right_down = pick_rows(down_right, factor_seeds[:, 3])
    buffer = lax.all_to_all(outgoing, ("ctx", "tp"), split_axis=0, concat_axis=0, tiled=True)
    up_act = jnp.einsum("slcd,ldh->slch", buffer, up_weight, preferred_element_type=jnp.float32)
    low_rank = jnp.einsum("slcd,ld->slc", buffer, left_up, preferred_element_type=jnp.float32)
    up_act = up_act + low_rank[..., None] * right_up[None, :, None, :].astype(jnp.float32)
    hidden = (jnp.maximum(up_act, 0.0) ** 2).astype(jnp.bfloat16)
    full_hidden = lax.all_gather(hidden, "exp", axis=3, tiled=True)
    summed = jnp.einsum(
        "slch,lhd->slcd", full_hidden, down_weight, preferred_element_type=jnp.float32
    )
    rank_sum = jnp.einsum(
        "slch,lh->slc", full_hidden, left_down, preferred_element_type=jnp.float32
    )
    result = (
        summed + rank_sum[..., None] * right_down[None, :, None, :].astype(jnp.float32)
    ).astype(jnp.bfloat16)
    returned = lax.all_to_all(result, ("ctx", "tp"), split_axis=0, concat_axis=0, tiled=True)
    back_rows = returned.reshape(experts_all * capacity, -1)
    picked = back_rows[target]
    normed = (route_gates / jnp.sum(route_gates, axis=1, keepdims=True)).reshape(-1)
    weighted = picked.astype(jnp.float32) * normed[:, None]
    moe_output = jnp.sum(weighted.reshape(tok_count, top_count, -1), axis=1)
    return moe_output.astype(jnp.bfloat16)


def solution(mesh):
    in_specs = (
        P(("pop", "ctx", "tp"), None),
        P(("pop", "ctx", "tp"), None),
        P(("pop", "ctx", "tp"), None),
        P(("ctx", "tp"), None, "exp"),
        P(("ctx", "tp"), None, "exp"),
        P(("pop", "ctx", "tp"), None),
        P(),
        P(None, "exp"),
        P(),
        P(None, "exp"),
    )
    out_specs = P(("pop", "ctx", "tp"), "exp")
    return jax.shard_map(
        on_device, mesh=mesh, in_specs=in_specs, out_specs=out_specs, check_vma=False
    )
```

profile of v0, /device:TPU:0, one launch (start us, length us, event | category | flops | bytes accessed | tf_op | source)
XLA Modules:
  0.0 316.2 jit_solution(15399134807292461094)
XLA Ops:
  6.5 0.8 copy.28
  7.4 0.1 eq.89
  7.5 0.1 eq.85
  7.6 0.7 broadcast_multiply_fusion
  8.4 1.7 reduce-window.6
  10.1 0.3 slice_reduce_fusion
  10.4 0.1 copy.27
  10.5 0.1 mul.56
  10.6 0.1 fusion.23
  10.7 3.4 %scatter_custom_fusion = s32[1024]{0:T(1024)S(1)} fusion(s32[768]{0:T(1024)S(1)} %fusion.33, s32[768]{0:T(1024)S(1)} %fusion.28, s32[]{:T(128)} %constant.11.clone.1), kind=kCustom, calls=%fused_computation.52 | custom fusion | bytes 4100 | tf_op jit(solution)/shard_map/scatter | solution.py:42
  14.1 1.2 concatenate.3
  15.3 6.6 %gather_fusion = bf16[1024,2688]{1,0:T(8,128)(2,1)} fusion(bf16[129,2688]{1,0:T(8,128)(2,1)S(1)} %concatenate.3, s32[1024]{0:T(1024)S(1)} %fusion.31), kind=kCustom, calls=%fused_computation | custom fusion | bytes 11014144 | tf_op jit(solution)/shard_map/gather | solution.py:45
  21.9 6.5 %all-to-all-start = ((bf16[8,2,64,2688]{3,2,1,0:T(8,128)(2,1)}), bf16[8,2,64,2688]{3,2,1,0:T(8,128)(2,1)}, u32[]{:S(2)}, u32[]{:S(2)}) async-start(bf16[8,2,64,2688]{3,2,1,0:T(8,128)(2,1)} %bitcast.67), calls=%async_computation | async-start | bytes 11010048 | tf_op jit(solution)/shard_map/all_to_all | solution.py:51
  28.4 0.2 slice_reduce_fusion.2
  28.7 0.2 fusion.10
  28.9 0.2 fusion.20
  29.1 121.5 %all-to-all-done = bf16[8,2,64,2688]{3,2,1,0:T(8,128)(2,1)} async-done(((bf16[8,2,64,2688]{3,2,1,0:T(8,128)(2,1)}), bf16[8,2,64,2688]{3,2,1,0:T(8,128)(2,1)}, u32[]{:S(2)}, u32[]{:S(2)}) %all-to-all-start) | async-done | bytes 5505056 | tf_op jit(solution)/shard_map/all_to_all | solution.py:51
  150.5 4.9 %fusion.5 = f32[2,1,8,64]{3,1,2,0:T(1,128)S(1)} fusion(bf16[8,2,64,2688]{3,2,1,0:T(8,128)(2,1)} %all-to-all-done, bf16[2,2688,1,1]{1,0,2,3:T(2,128)(2,1)S(1)} %fusion.10), kind=kOutput, calls=%fused_computation.10 | convolution fusion | flops 5505024 | bytes 5519872 | tf_op jit(solution)/shard_map/slcd,ld->slc/dot_general | solution.py:53
  155.4 10.8 %fusion.13 = bf16[8,2,64,768]{3,2,0,1:T(8,128)(2,1)} fusion(bf16[2,2688,768]{2,1,0:T(8,128)(2,1)} %param.13, bf16[8,2,64,2688]{3,2,1,0:T(8,128)(2,1)} %all-to-all-done, f32[2,768]{1,0:T(2,128)S(1)} %fusion.20, f32[8,2,64]{2,0,1:T(8,128)S(1)} %bitcast.70), kind=kOutput, calls=%fused_computation.18 | convolution fusion | flops 4231790592 | bytes 15345664 | tf_op jit(solution)/shard_map/slcd,ldh->slch/dot_general | solution.py:52
  166.3 0.2 fusion.15
  166.5 0.2 fusion.14
  166.7 43.6 %all-gather.2.cloned.1.call-done = bf16[8,2,64,1536]{3,2,0,1:T(8,128)(2,1)} async-done(((bf16[8,2,64,768]{3,2,0,1:T(8,128)(2,1)}), bf16[8,2,64,1536]{3,2,0,1:T(8,128)(2,1)}) %all-gather.2.cloned.1.call-update) | async-done | bytes 3145744 | tf_op jit(solution)/shard_map/all_gather | solution.py:56
  210.3 3.2 %fusion.26 = f32[2,1,8,64]{3,1,2,0:T(1,128)S(1)} fusion(bf16[8,2,64,1536]{3,2,0,1:T(8,128)(2,1)} %all-gather.2.cloned.1.call-done, bf16[2,1536,1,1]{1,0,2,3:T(2,128)(2,1)S(1)} %fusion.15), kind=kOutput, calls=%fused_computation.36 | convolution fusion | flops 3145728 | bytes 3155968 | tf_op jit(solution)/shard_map/slch,lh->slc/dot_general | solution.py:60
  213.5 9.2 %fusion.4 = bf16[8,2,64,1344]{3,2,0,1:T(8,128)(2,1)S(1)} fusion(bf16[8,2,64,1536]{3,2,0,1:T(8,128)(2,1)} %all-gather.2.cloned.1.call-done, bf16[2,1536,1344]{1,2,0:T(8,128)(2,1)} %param.14, f32[2,1344]{1,0:T(2,128)S(1)} %fusion.14, f32[8,2,64]{2,0,1:T(8,128)S(1)} %bitcast.69), kind=kOutput, calls=%fused_computation.8 | convolution fusion | flops 4231987200 | bytes 14170624 | tf_op jit(solution)/shard_map/slch,lhd->slcd/dot_general | solution.py:57
  222.7 1.8 copy.32
  224.5 4.6 %all-to-all-start.1 = ((bf16[8,2,64,1344]{3,2,1,0:T(8,128)(2,1)}), bf16[8,2,64,1344]{3,2,1,0:T(8,128)(2,1)S(1)}, u32[]{:S(2)}, u32[]{:S(2)}) async-start(bf16[8,2,64,1344]{3,2,1,0:T(8,128)(2,1)} %copy.32), calls=%async_computation.1 | async-start | bytes 5767168 | tf_op jit(solution)/shard_map/all_to_all | solution.py:66
  229.1 0.1 copy.33
  229.3 65.7 %all-to-all-done.1 = bf16[8,2,64,1344]{3,2,1,0:T(8,128)(2,1)S(1)} async-done(((bf16[8,2,64,1344]{3,2,1,0:T(8,128)(2,1)}), bf16[8,2,64,1344]{3,2,1,0:T(8,128)(2,1)S(1)}, u32[]{:S(2)}, u32[]{:S(2)}) %all-to-all-start.1) | async-done | bytes 2752544 | tf_op jit(solution)/shard_map/all_to_all | solution.py:66
  295.0 3.7 %gather_fusion.1 = bf16[768,1344]{1,0:T(8,128)(2,1)} fusion(bf16[1024,1344]{1,0:T(8,128)(2,1)S(1)} %bitcast.66, s32[1024]{0:T(1024)S(1)} %pad_clamp_fusion), kind=kCustom, calls=%fused_computation.1 | custom fusion | bytes 4131840 | tf_op jit(solution)/shard_map/gather | solution.py:68
  298.7 5.0 %reshape.72 = f32[128,6,1344]{2,1,0:T(8,128)} reshape(bf16[768,1344]{1,0:T(8,128)(2,1)} %gather_fusion.1) | data formatting | bytes 6193152 | tf_op jit(solution)/shard_map/convert_element_type | solution.py:70
  303.7 4.7 %multiply_reduce_fusion = bf16[128,1344]{1,0:T(8,128)(2,1)S(1)} fusion(f32[128,6,1344]{2,1,0:T(8,128)} %reshape.72, f32[128,6]{1,0:T(8,128)S(1)} %copy.33), kind=kLoop, calls=%fused_computation.9 | loop fusion | flops 1892352 | bytes 4475904 | tf_op jit(solution)/shard_map/reduce_sum | solution.py:71
  308.5 0.9 copy.34
  (22 shorter events, 0.2 us)
Async XLA Ops:
  6.5 22.1 %copy-start = (bf16[16,2688]{1,0:T(8,128)(2,1)S(1)}, bf16[16,2688]{1,0:T(8,128)(2,1)}, u32[]{:S(2)}) copy-start(bf16[16,2688]{1,0:T(8,128)(2,1)} %param.16) | copy-start | bytes 258052
  21.9 6.5 %copy-start.2 = (s32[2,4]{1,0:T(2,128)S(1)}, s32[2,4]{1,0:T(2,128)}, u32[]{:S(2)}) copy-start(s32[2,4]{1,0:T(2,128)} %param.15) | copy-start | bytes 100
  21.9 7.0 %copy-start.5 = (bf16[16,768]{1,0:T(8,128)(2,1)S(1)}, bf16[16,768]{1,0:T(8,128)(2,1)}, u32[]{:S(2)}) copy-start(bf16[16,768]{1,0:T(8,128)(2,1)} %param.17) | copy-start | bytes 73732
  21.9 128.7 %all-to-all-start = ((bf16[8,2,64,2688]{3,2,1,0:T(8,128)(2,1)}), bf16[8,2,64,2688]{3,2,1,0:T(8,128)(2,1)}, u32[]{:S(2)}, u32[]{:S(2)}) async-start(bf16[8,2,64,2688]{3,2,1,0:T(8,128)(2,1)} %bitcast.67), calls=%async_computation | async-start | bytes 11010048 | tf_op jit(solution)/shard_map/all_to_all | solution.py:51
  28.4 181.9 %all-gather.2.cloned.1.call-start = ((), (), s32[]{:S(2)}) async-start(), calls=%async_computation.2 | async-start | bytes 4718592 | tf_op jit(solution)/shard_map/all_gather | solution.py:56
  155.4 10.9 %copy-start.3 = (bf16[16,1536]{1,0:T(8,128)(2,1)S(1)}, bf16[16,1536]{1,0:T(8,128)(2,1)}, u32[]{:S(2)}) copy-start(bf16[16,1536]{1,0:T(8,128)(2,1)} %param.18) | copy-start | bytes 147460
  155.4 11.1 %copy-start.4 = (bf16[16,1344]{1,0:T(8,128)(2,1)S(1)}, bf16[16,1344]{1,0:T(8,128)(2,1)}, u32[]{:S(2)}) copy-start(bf16[16,1344]{1,0:T(8,128)(2,1)} %param.19) | copy-start | bytes 129028
  222.7 6.4 %copy-start.1 = (f32[128,6]{0,1:T(8,128)S(1)}, f32[128,6]{0,1:T(8,128)}, u32[]{:S(2)}) copy-start(f32[128,6]{0,1:T(8,128)} %param.12) | copy-start | bytes 9220
  224.5 70.5 %all-to-all-start.1 = ((bf16[8,2,64,1344]{3,2,1,0:T(8,128)(2,1)}), bf16[8,2,64,1344]{3,2,1,0:T(8,128)(2,1)S(1)}, u32[]{:S(2)}, u32[]{:S(2)}) async-start(bf16[8,2,64,1344]{3,2,1,0:T(8,128)(2,1)} %copy.32), calls=%async_computation.1 | async-start | bytes 5767168 | tf_op jit(solution)/shard_map/all_to_all | solution.py:66
Sparse Core Ops, SparseCore 0:
  166.4 43.8 all-gather.1
where the time goes:
time: 317 us; the launch traced here: 316 us
  waiting for transfers between devices  231 us (73%)
  matrix products  28.9 us (9%)
  local copies, waits for them, and re-layouts  24.5 us (8%)
  between operations  13.5 us (4%)
  starting transfers between devices  11.1 us (4%)
  other arithmetic  7.34 us (2%)
    all_to_all x1, waiting for transfers between devices, on_device(): lax.all_to_all(outgoing, ('ctx', 'tp'), split_axis=0, concat_axis=0, tile...  121 us
    all_to_all x1, waiting for transfers between devices, on_device(): lax.all_to_all(result, ('ctx', 'tp'), split_axis=0, concat_axis=0, tiled=...  65.7 us
    all_gather x1, waiting for transfers between devices, on_device(): full_hidden = lax.all_gather(hidden, 'exp', axis=3, tiled=True)  43.6 us
    dot_general x1, matrix products, on_device(): jnp.einsum('slcd,ldh->slch', buffer, up_weight, preferred_element_type=jn...  10.8 us
    dot_general x1, matrix products, on_device(): jnp.einsum('slch,lhd->slcd', full_hidden, down_weight, preferred_element_...  9.17 us
    gather x1, local copies, waits for them, and re-layouts, on_device(): token_rows = padded_tokens[source_row]  6.58 us
    all_to_all x1, starting transfers between devices, on_device(): lax.all_to_all(outgoing, ('ctx', 'tp'), split_axis=0, concat_axis=0, tile...  6.49 us
  transfers between devices with their start and end apart: 3, of which 3 were waited for; matrix products, arithmetic and copies ran while one was open for 0% of the time, Pallas kernels for 0%

commit v1 on v0

--- a/solution.py
+++ b/solution.py
@@ -53,7 +53,16 @@
     low_rank = jnp.einsum("slcd,ld->slc", buffer, left_up, preferred_element_type=jnp.float32)
     up_act = up_act + low_rank[..., None] * right_up[None, :, None, :].astype(jnp.float32)
     hidden = (jnp.maximum(up_act, 0.0) ** 2).astype(jnp.bfloat16)
-    full_hidden = lax.all_gather(hidden, "exp", axis=3, tiled=True)
+    place_types_over_axis = lambda work_x: jnp.concatenate(
+        lax.all_to_all(
+            jnp.stack([work_x for _ in range(lax.axis_size("exp"))], axis=0),
+            "exp",
+            split_axis=0,
+            concat_axis=0,
+        ),
+        axis=3,
+    )
+    full_hidden = place_types_over_axis(hidden)
     summed = jnp.einsum(
         "slch,lhd->slcd", full_hidden, down_weight, preferred_element_type=jnp.float32
     )

time: 317 us -> 297 us (0.937)
  between operations: 13.5 us -> 0.17 us
  waiting for transfers between devices: 231 us -> 223 us
  matrix products: 28.9 us -> 25.3 us
  starting transfers between devices: 11.1 us -> 14.5 us
    all_gather x1 -> x0, waiting for transfers between devices: 43.6 us -> none  [on_device(): full_hidden = lax.all_gather(hidden, 'exp', axis=3, tiled=True)]
    all_to_all x0 -> x1, waiting for transfers between devices: none -> 35.6 us  [on_device(): lax.all_to_all(jnp.stack([work_x for _ in range(lax.axis_size('exp'))], a...]
    all_to_all x0 -> x1, starting transfers between devices: none -> 4.08 us  [on_device(): lax.all_to_all(jnp.stack([work_x for _ in range(lax.axis_size('exp'))], a...]
where the time goes in v1:
time: 297 us
  waiting for transfers between devices  223 us (75%)
  matrix products  25.3 us (9%)
  local copies, waits for them, and re-layouts  24.8 us (8%)
  starting transfers between devices  14.5 us (5%)
  other arithmetic  9.28 us (3%)
    all_to_all x1, waiting for transfers between devices, on_device(): lax.all_to_all(outgoing, ('ctx', 'tp'), split_axis=0, concat_axis=0, tile...  122 us
    all_to_all x1, waiting for transfers between devices, on_device(): lax.all_to_all(result, ('ctx', 'tp'), split_axis=0, concat_axis=0, tiled=...  65.5 us
    all_to_all x1, waiting for transfers between devices, on_device(): lax.all_to_all(jnp.stack([work_x for _ in range(lax.axis_size('exp'))], a...  35.6 us
    dot_general x1, matrix products, on_device(): jnp.einsum('slcd,ldh->slch', buffer, up_weight, preferred_element_type=jn...  9.66 us
    dot_general x1, matrix products, on_device(): jnp.einsum('slch,lhd->slcd', full_hidden, down_weight, preferred_element_...  8.67 us
    gather x1, local copies, waits for them, and re-layouts, on_device(): token_rows = padded_tokens[source_row]  6.58 us
    all_to_all x1, starting transfers between devices, on_device(): lax.all_to_all(outgoing, ('ctx', 'tp'), split_axis=0, concat_axis=0, tile...  6.49 us
  transfers between devices with their start and end apart: 3, of which 3 were waited for; matrix products, arithmetic and copies ran while one was open for 0% of the time, Pallas kernels for 0%

profile of v1, /device:TPU:0, one launch (start us, length us, event | category | flops | bytes accessed | tf_op | source)
XLA Modules:
  0.0 296.7 jit_solution(13548926594514431275)
XLA Ops:
  0.0 0.8 copy.32
  0.8 0.1 eq.89
  1.0 0.1 eq.85
  1.1 0.7 broadcast_multiply_fusion
  1.8 1.7 reduce-window.6
  3.5 0.3 slice_reduce_fusion
  3.9 0.1 mul.56
  4.2 3.4 %scatter_custom_fusion = s32[1024]{0:T(1024)S(1)} fusion(s32[768]{0:T(1024)S(1)} %fusion.38, s32[768]{0:T(1024)S(1)} %fusion.33, s32[]{:T(128)} %constant.11.clone.1), kind=kCustom, calls=%fused_computation.54 | custom fusion | bytes 4100 | tf_op jit(solution)/shard_map/scatter | solution.py:42
  7.6 1.2 concatenate.3
  8.8 6.6 %gather_fusion = bf16[1024,2688]{1,0:T(8,128)(2,1)} fusion(bf16[129,2688]{1,0:T(8,128)(2,1)S(1)} %concatenate.3, s32[1024]{0:T(1024)S(1)} %fusion.36), kind=kCustom, calls=%fused_computation | custom fusion | bytes 11014144 | tf_op jit(solution)/shard_map/gather | solution.py:45
  15.3 6.5 %all-to-all-start = ((bf16[8,2,64,2688]{3,2,1,0:T(8,128)(2,1)}), bf16[8,2,64,2688]{3,2,1,0:T(8,128)(2,1)}, u32[]{:S(2)}, u32[]{:S(2)}) async-start(bf16[8,2,64,2688]{3,2,1,0:T(8,128)(2,1)} %bitcast.76), calls=%async_computation | async-start | bytes 11010048 | tf_op jit(solution)/shard_map/all_to_all | solution.py:51
  21.8 0.2 slice_reduce_fusion.2
  22.1 0.2 fusion.10
  22.3 0.2 fusion.25
  22.5 121.5 %all-to-all-done = bf16[8,2,64,2688]{3,2,1,0:T(8,128)(2,1)} async-done(((bf16[8,2,64,2688]{3,2,1,0:T(8,128)(2,1)}), bf16[8,2,64,2688]{3,2,1,0:T(8,128)(2,1)}, u32[]{:S(2)}, u32[]{:S(2)}) %all-to-all-start) | async-done | bytes 5505056 | tf_op jit(solution)/shard_map/all_to_all | solution.py:51
  144.0 4.9 %fusion.5 = f32[2,1,8,64]{3,1,2,0:T(1,128)S(1)} fusion(bf16[8,2,64,2688]{3,2,1,0:T(8,128)(2,1)} %all-to-all-done, bf16[2,2688,1,1]{1,0,2,3:T(2,128)(2,1)S(1)} %fusion.10), kind=kOutput, calls=%fused_computation.10 | convolution fusion | flops 5505024 | bytes 5519872 | tf_op jit(solution)/shard_map/slcd,ld->slc/dot_general | solution.py:53
  148.9 9.7 %fusion.20 = bf16[1,8,2,64,768]{4,3,1,2,0:T(8,128)(2,1)S(1)} fusion(f32[2,768]{1,0:T(2,128)S(1)} %fusion.25, f32[8,2,64]{2,0,1:T(8,128)S(1)} %bitcast.82, bf16[2,2688,768]{2,1,0:T(8,128)(2,1)} %param.13, bf16[8,2,64,2688]{3,2,1,0:T(8,128)(2,1)} %all-to-all-done), kind=kOutput, calls=%fused_computation.24 | convolution fusion | flops 4231790592 | bytes 15345664 | tf_op jit(solution)/shard_map/slcd,ldh->slch/dot_general | solution.py:52
  158.6 1.9 pad_maximum_fusion
  160.5 4.1 %all-to-all-start.1 = ((bf16[2,8,2,64,768]{4,3,1,2,0:T(8,128)(2,1)}), bf16[2,8,2,64,768]{4,3,1,2,0:T(8,128)(2,1)S(1)}, u32[]{:S(2)}, u32[]{:S(2)}) async-start(bf16[2,8,2,64,768]{4,3,1,2,0:T(8,128)(2,1)} %pad_maximum_fusion), calls=%async_computation.1 | async-start | bytes 6291456 | tf_op jit(solution)/shard_map/all_to_all | solution.py:57
  164.6 0.2 fusion.15
  164.8 0.2 fusion.14
  165.0 35.6 %all-to-all-done.1 = bf16[2,8,2,64,768]{4,3,1,2,0:T(8,128)(2,1)S(1)} async-done(((bf16[2,8,2,64,768]{4,3,1,2,0:T(8,128)(2,1)}), bf16[2,8,2,64,768]{4,3,1,2,0:T(8,128)(2,1)S(1)}, u32[]{:S(2)}, u32[]{:S(2)}) %all-to-all-start.1) | async-done | bytes 3145760 | tf_op jit(solution)/shard_map/all_to_all | solution.py:57
  200.6 0.3 copy.50
  200.9 1.3 fusion.31
  202.2 8.7 %fusion.4 = bf16[8,2,64,1344]{3,2,0,1:T(8,128)(2,1)S(1)} fusion(bf16[8,2,64,1536]{3,2,0,1:T(8,128)(2,1)S(1)} %bitcast.79, bf16[2,1536,1344]{1,2,0:T(8,128)(2,1)} %param.14, f32[2,1344]{1,0:T(2,128)S(1)} %fusion.14, f32[8,2,64]{2,0,1:T(8,128)S(1)} %bitcast.81), kind=kOutput, calls=%fused_computation.8 | convolution fusion | flops 4231987200 | bytes 14170624 | tf_op jit(solution)/shard_map/slch,lhd->slcd/dot_general | solution.py:66
  210.9 1.8 copy.38
  212.7 3.9 %all-to-all-start.2 = ((bf16[8,2,64,1344]{3,2,1,0:T(8,128)(2,1)}), bf16[8,2,64,1344]{3,2,1,0:T(8,128)(2,1)S(1)}, u32[]{:S(2)}, u32[]{:S(2)}) async-start(bf16[8,2,64,1344]{3,2,1,0:T(8,128)(2,1)} %copy.38), calls=%async_computation.2 | async-start | bytes 5767168 | tf_op jit(solution)/shard_map/all_to_all | solution.py:75
  216.8 65.5 %all-to-all-done.2 = bf16[8,2,64,1344]{3,2,1,0:T(8,128)(2,1)S(1)} async-done(((bf16[8,2,64,1344]{3,2,1,0:T(8,128)(2,1)}), bf16[8,2,64,1344]{3,2,1,0:T(8,128)(2,1)S(1)}, u32[]{:S(2)}, u32[]{:S(2)}) %all-to-all-start.2) | async-done | bytes 2752544 | tf_op jit(solution)/shard_map/all_to_all | solution.py:75
  282.3 3.7 %gather_fusion.1 = bf16[768,1344]{1,0:T(8,128)(2,1)} fusion(bf16[1024,1344]{1,0:T(8,128)(2,1)S(1)} %bitcast.75, s32[1024]{0:T(1024)S(1)} %pad_clamp_fusion), kind=kCustom, calls=%fused_computation.1 | custom fusion | bytes 4131840 | tf_op jit(solution)/shard_map/gather | solution.py:77
  286.0 5.0 %reshape.80 = f32[128,6,1344]{2,1,0:T(8,128)} reshape(bf16[768,1344]{1,0:T(8,128)(2,1)} %gather_fusion.1) | data formatting | bytes 6193152 | tf_op jit(solution)/shard_map/convert_element_type | solution.py:79
  291.0 4.7 %multiply_reduce_fusion = bf16[128,1344]{1,0:T(8,128)(2,1)S(1)} fusion(f32[128,6,1344]{2,1,0:T(8,128)} %reshape.80, f32[128,6]{1,0:T(8,128)S(1)} %copy.39), kind=kLoop, calls=%fused_computation.9 | loop fusion | flops 1892352 | bytes 4475904 | tf_op jit(solution)/shard_map/reduce_sum | solution.py:80
  295.8 0.9 copy.40
  (23 shorter events, 0.4 us)
Async XLA Ops:
  0.0 22.1 %copy-start = (bf16[16,2688]{1,0:T(8,128)(2,1)S(1)}, bf16[16,2688]{1,0:T(8,128)(2,1)}, u32[]{:S(2)}) copy-start(bf16[16,2688]{1,0:T(8,128)(2,1)} %param.16) | copy-start | bytes 258052
  15.3 6.5 %copy-start.2 = (s32[2,4]{1,0:T(2,128)S(1)}, s32[2,4]{1,0:T(2,128)}, u32[]{:S(2)}) copy-start(s32[2,4]{1,0:T(2,128)} %param.15) | copy-start | bytes 100
  15.3 6.9 %copy-start.5 = (bf16[16,768]{1,0:T(8,128)(2,1)S(1)}, bf16[16,768]{1,0:T(8,128)(2,1)}, u32[]{:S(2)}) copy-start(bf16[16,768]{1,0:T(8,128)(2,1)} %param.17) | copy-start | bytes 73732
  15.3 128.7 %all-to-all-start = ((bf16[8,2,64,2688]{3,2,1,0:T(8,128)(2,1)}), bf16[8,2,64,2688]{3,2,1,0:T(8,128)(2,1)}, u32[]{:S(2)}, u32[]{:S(2)}) async-start(bf16[8,2,64,2688]{3,2,1,0:T(8,128)(2,1)} %bitcast.76), calls=%async_computation | async-start | bytes 11010048 | tf_op jit(solution)/shard_map/all_to_all | solution.py:51
  160.5 4.1 %copy-start.3 = (bf16[16,1536]{1,0:T(8,128)(2,1)S(1)}, bf16[16,1536]{1,0:T(8,128)(2,1)}, u32[]{:S(2)}) copy-start(bf16[16,1536]{1,0:T(8,128)(2,1)} %param.18) | copy-start | bytes 147460
  160.5 4.3 %copy-start.4 = (bf16[16,1344]{1,0:T(8,128)(2,1)S(1)}, bf16[16,1344]{1,0:T(8,128)(2,1)}, u32[]{:S(2)}) copy-start(bf16[16,1344]{1,0:T(8,128)(2,1)} %param.19) | copy-start | bytes 129028
  160.5 40.1 %all-to-all-start.1 = ((bf16[2,8,2,64,768]{4,3,1,2,0:T(8,128)(2,1)}), bf16[2,8,2,64,768]{4,3,1,2,0:T(8,128)(2,1)S(1)}, u32[]{:S(2)}, u32[]{:S(2)}) async-start(bf16[2,8,2,64,768]{4,3,1,2,0:T(8,128)(2,1)} %pad_maximum_fusion), calls=%async_computation.1 | async-start | bytes 6291456 | tf_op jit(solution)/shard_map/all_to_all | solution.py:57
  212.7 4.0 %copy-start.1 = (f32[128,6]{0,1:T(8,128)S(1)}, f32[128,6]{0,1:T(8,128)}, u32[]{:S(2)}) copy-start(f32[128,6]{0,1:T(8,128)} %param.12) | copy-start | bytes 9220
  212.7 69.6 %all-to-all-start.2 = ((bf16[8,2,64,1344]{3,2,1,0:T(8,128)(2,1)}), bf16[8,2,64,1344]{3,2,1,0:T(8,128)(2,1)S(1)}, u32[]{:S(2)}, u32[]{:S(2)}) async-start(bf16[8,2,64,1344]{3,2,1,0:T(8,128)(2,1)} %copy.38), calls=%async_computation.2 | async-start | bytes 5767168 | tf_op jit(solution)/shard_map/all_to_all | solution.py:75
